TPU v7x, 512 devices: a whole 4x8x8 slice. The times are simulated.
512 devices in a mesh: round: 128 (over z, y, core), mp: 4 (over x).
Axes of the slice: x: 4, y: 8, z: 8, core: 2. Of those that a mesh axis runs over, the one named last changes fastest.
Arguments:
- tokens: bfloat16 [128, 512, 512], P('round'), may hold values from -8 to 8
- cell_order: int32 [512], replicated, may hold values from 0 to 511, each once
- seam_rows: int32 [128, 128, 2], P('round'), may hold values from -1 to 511, as said below
- obs_mask: int32 [16, 512], replicated, may hold values from 0 to 1, as said below
- norm_gain: float32 [512], replicated, may hold values from 0.1 to 1.9
- w_query: bfloat16 [512, 512], P(None, 'mp'), may hold values from -1 to 1
- w_key: bfloat16 [512, 512], P(None, 'mp'), may hold values from -1 to 1
- w_value: bfloat16 [512, 512], P(None, 'mp'), may hold values from -0.25 to 0.25
- w_out: bfloat16 [512, 512], P('mp'), may hold values from -0.25 to 0.25
- w_gate: bfloat16 [512, 2048], P(None, 'mp'), may hold values from -0.25 to 0.25
- w_up: bfloat16 [512, 2048], P(None, 'mp'), may hold values from -0.25 to 0.25
- w_down: bfloat16 [2048, 512], P('mp'), may hold values from -0.125 to 0.125
- w_read: float32 [512], replicated, may hold values from -0.25 to 0.25
Outputs:
- tiles_out: bfloat16 [128, 512, 512], P('mp', 'round')
- obs_logits: float32 [16], replicated
Inputs may be any that keep to these rules, and one draw needn't show every extreme that they name: `seam_rows`: each entry is a row of the sending tile or -1 for an empty slot; the live entries of one tile are all different; a tile's slots to itself are full, and some owner's slots are full from every tile. `obs_mask`: every observable's support holds at least one cell.
All inputs are finite; a program needn't handle non-finite values.
Results may differ from a plain program's by a relative error of at most 0.0052.
The roundings to bfloat16 on the way count: a program that leaves them out, or rounds other values in their place, can miss the bound.
Values may be sent and summed in bfloat16 or wider, within the bound.
A program may use at most 64 MiB of HBM per device.

v0:
```python
import math
import jax
import jax.numpy as jnp
from jax import lax
from jax.sharding import PartitionSpec as P

HDIM = 64
norm_eps = 1e-06


def normalize(rows_in, norm_gain):
    values = rows_in.astype(jnp.float32)
    spread = jnp.mean(values * values, axis=-1, keepdims=True)
    return (values * lax.rsqrt(spread + norm_eps) * norm_gain).astype(jnp.bfloat16)


def attend(queries, keys_all, values_all, live_keys):
    scale_factor = 1.0 / math.sqrt(queries.shape[-1])
    scores = (
        jnp.einsum("qhe,khe->hqk", queries, keys_all, preferred_element_type=jnp.float32)
        * scale_factor
    )
    if live_keys is not None:
        scores = jnp.where(live_keys[None, None, :], scores, -1e30)
    row_max = jnp.max(scores, axis=-1, keepdims=True)
    weights = jnp.exp(scores - row_max)
    probabilities = (weights / jnp.sum(weights, axis=-1, keepdims=True)).astype(jnp.bfloat16)
    mixture = jnp.einsum(
        "hqk,khe->qhe", probabilities, values_all, preferred_element_type=jnp.float32
    )
    return mixture.reshape(mixture.shape[0], -1)


def shards(
    tokens,
    cell_order,
    seam_rows,
    obs_mask,
    norm_gain,
    w_query,
    w_key,
    w_value,
    w_out,
    w_gate,
    w_up,
    w_down,
    w_read,
):
    round_count = lax.axis_size("round")
    model_count = lax.axis_size("mp")
    model_index = lax.axis_index("mp")
    round_index = lax.axis_index("round")
    width = tokens.shape[2]
    cell_dev = tokens.shape[1] // round_count
    permuted = tokens[:, cell_order, :]
    tile_tokens = lax.all_to_all(permuted, "round", split_axis=1, concat_axis=0, tiled=True)
    tile_rows = tile_tokens.shape[0] * cell_dev
    flat_tokens = tile_tokens.reshape(tile_rows, width)
    normed = normalize(flat_tokens, norm_gain)
    queries = jnp.dot(normed, w_query, preferred_element_type=jnp.float32).astype(jnp.bfloat16)
    keys_all = jnp.dot(normed, w_key, preferred_element_type=jnp.float32).astype(jnp.bfloat16)
    values_all = jnp.dot(normed, w_value, preferred_element_type=jnp.float32).astype(jnp.bfloat16)
    head_width = queries.shape[1]
    heads_dev = head_width // HDIM
    block_rows = min(512, tile_rows)
    query_blocks = queries.reshape(tile_rows // block_rows, block_rows, heads_dev, HDIM)
    key_heads = keys_all.reshape(tile_rows, heads_dev, HDIM)
    value_heads = values_all.reshape(tile_rows, heads_dev, HDIM)
    local_attn = lax.map(
        lambda query_block: attend(query_block, key_heads, value_heads, None), query_blocks
    )
    local_attn = local_attn.reshape(tile_rows, head_width)
    live_slot = seam_rows[0] >= 0
    safe_rows = jnp.where(live_slot, seam_rows[0], 0)
    packet = (
        lax.all_to_all(queries[safe_rows], "round", split_axis=0, concat_axis=0, tiled=True),
        lax.all_to_all(keys_all[safe_rows], "round", split_axis=0, concat_axis=0, tiled=True),
        lax.all_to_all(values_all[safe_rows], "round", split_axis=0, concat_axis=0, tiled=True),
        lax.all_to_all(
            live_slot.astype(jnp.bfloat16), "round", split_axis=0, concat_axis=0, tiled=True
        ),
    )
    seam_queries = packet[0].reshape(-1, heads_dev, HDIM)
    seam_keys = packet[1].reshape(-1, heads_dev, HDIM)
    seam_values = packet[2].reshape(-1, heads_dev, HDIM)
    seam_live = packet[3].reshape(-1) > 0.5
    seam_attn = attend(seam_queries, seam_keys, seam_values, seam_live).astype(jnp.bfloat16)
    returned = lax.all_to_all(
        seam_attn.reshape(round_count, -1, head_width),
        "round",
        split_axis=0,
        concat_axis=0,
        tiled=True,
    )
    target = jnp.where(live_slot, seam_rows[0], tile_rows).reshape(-1)
    combined = (
        local_attn.at[target]
        .add(returned.reshape(-1, head_width).astype(jnp.float32), mode="drop")
        .astype(jnp.bfloat16)
    )
    share_rows = tile_rows // model_count
    own_first = model_index * share_rows
    gate_part = jnp.dot(normed, w_gate, preferred_element_type=jnp.float32)
    up_part = jnp.dot(normed, w_up, preferred_element_type=jnp.float32)
    hidden = (jax.nn.silu(gate_part) * up_part).astype(jnp.bfloat16)
    attn_part = jnp.dot(combined, w_out, preferred_element_type=jnp.float32)
    summed = lax.psum_scatter(
        attn_part + jnp.dot(hidden, w_down, preferred_element_type=jnp.float32),
        "mp",
        scatter_dimension=0,
        tiled=True,
    )
    own_rows = lax.dynamic_slice_in_dim(flat_tokens, own_first, share_rows, 0)
    result_rows = (own_rows.astype(jnp.float32) + summed).astype(jnp.bfloat16)
    tiles_out = result_rows.reshape(share_rows // cell_dev, cell_dev, width)
    my_cells = lax.dynamic_slice_in_dim(cell_order, round_index * cell_dev, cell_dev)
    support = obs_mask[:, my_cells].astype(jnp.float32)
    partial_sum = jnp.einsum(
        "oc,rcd->od", support, tiles_out.astype(jnp.float32), precision=lax.Precision.HIGHEST
    )
    support_count = round_count * jnp.sum(obs_mask.astype(jnp.float32), axis=1)
    divisor = jnp.sqrt(support_count)
    pooled = lax.psum(partial_sum, ("round", "mp"))
    obs_logits = jnp.dot(pooled, w_read, precision=lax.Precision.HIGHEST) / divisor
    return (tiles_out, obs_logits)


def solution(mesh):
    return jax.shard_map(
        shards,
        mesh=mesh,
        in_specs=(
            P("round", None, None),
            P(),
            P("round", None, None),
            P(),
            P(),
            P(None, "mp"),
            P(None, "mp"),
            P(None, "mp"),
            P("mp", None),
            P(None, "mp"),
            P(None, "mp"),
            P("mp", None),
            P(),
        ),
        out_specs=(P("mp", "round", None), P()),
        check_vma=False,
    )
```

profile of v0, /device:TPU:1, one launch (start us, length us, event | category | flops | bytes accessed | tf_op | source)
XLA Modules:
  0.0 291.0 jit_solution(16656046799085090074)
XLA Ops:
  8.7 18.4 %all-to-all-start.2 = ((bf16[128,1,2]{2,1,0:T(2,128)(2,1)}), bf16[128,1,2]{2,1,0:T(2,128)(2,1)S(1)}, u32[]{:S(2)}, u32[]{:S(2)}) async-start(bf16[128,1,2]{2,1,0:T(2,128)(2,1)} %copy.61), calls=%async_computation.2 | async-start | bytes 131072 | tf_op jit(solution)/shard_map/all_to_all | solution.py:79
  27.8 2.0 gather_fusion
  31.1 3.8 %reduce.2 = bf16[512,512]{1,0:T(8,128)(2,1)S(1)} reduce(bf16[512,1,512]{2,1,0:T(2,128)(2,1)S(1)} %bitcast.69, bf16[]{:T(256)} %broadcast.153), dimensions={1}, to_apply=%bitcast.66.reduce_sub_computation | reduce | bytes 1048578
  35.0 1.1 reshape.218
  36.1 2.4 all-to-all-done.2
  38.5 11.3 %all-to-all-start = ((bf16[128,2,1024]{2,1,0:T(2,128)(2,1)}), bf16[128,2,1024]{2,1,0:T(2,128)(2,1)S(1)}, u32[]{:S(2)}, u32[]{:S(2)}) async-start(bf16[128,2,1024]{2,1,0:T(2,128)(2,1)} %reshape.218), calls=%async_computation | async-start | bytes 1048576 | tf_op jit(solution)/shard_map/all_to_all | solution.py:56
  50.8 19.6 %all-to-all-done = bf16[128,2,1024]{2,1,0:T(2,128)(2,1)S(1)} async-done(((bf16[128,2,1024]{2,1,0:T(2,128)(2,1)}), bf16[128,2,1024]{2,1,0:T(2,128)(2,1)S(1)}, u32[]{:S(2)}, u32[]{:S(2)}) %all-to-all-start) | async-done | bytes 524320 | tf_op jit(solution)/shard_map/all_to_all | solution.py:56
  70.9 1.1 bitcast_convert_fusion
  74.1 1.5 gather_fusion.1
  75.6 1.5 gather_fusion.2
  77.0 6.3 %all-to-all-start.3 = ((bf16[128,2,128]{2,1,0:T(2,128)(2,1)}), bf16[128,2,128]{2,1,0:T(2,128)(2,1)}, u32[]{:S(2)}, u32[]{:S(2)}) async-start(bf16[128,2,128]{2,1,0:T(2,128)(2,1)} %bitcast.12), calls=%async_computation.3 | async-start | bytes 131072 | tf_op jit(solution)/shard_map/all_to_all | solution.py:76
  83.3 1.5 fusion.55
  86.8 1.5 gather_fusion.3
  88.3 5.8 %all-to-all-done.3 = bf16[128,2,128]{2,1,0:T(2,128)(2,1)} async-done(((bf16[128,2,128]{2,1,0:T(2,128)(2,1)}), bf16[128,2,128]{2,1,0:T(2,128)(2,1)}, u32[]{:S(2)}, u32[]{:S(2)}) %all-to-all-start.3) | async-done | bytes 65568 | tf_op jit(solution)/shard_map/all_to_all | solution.py:76
  94.1 8.0 %all-to-all-start.4 = ((bf16[128,2,128]{2,1,0:T(2,128)(2,1)}), bf16[128,2,128]{2,1,0:T(2,128)(2,1)}, u32[]{:S(2)}, u32[]{:S(2)}) async-start(bf16[128,2,128]{2,1,0:T(2,128)(2,1)} %bitcast.78), calls=%async_computation.4 | async-start | bytes 131072 | tf_op jit(solution)/shard_map/all_to_all | solution.py:77
  102.1 1.7 fusion.49
  104.8 8.5 %all-to-all-done.4 = bf16[128,2,128]{2,1,0:T(2,128)(2,1)} async-done(((bf16[128,2,128]{2,1,0:T(2,128)(2,1)}), bf16[128,2,128]{2,1,0:T(2,128)(2,1)}, u32[]{:S(2)}, u32[]{:S(2)}) %all-to-all-start.4) | async-done | bytes 65568 | tf_op jit(solution)/shard_map/all_to_all | solution.py:77
  113.3 6.9 %all-to-all-start.1 = ((bf16[128,2,128]{2,1,0:T(2,128)(2,1)}), bf16[128,2,128]{2,1,0:T(2,128)(2,1)}, u32[]{:S(2)}, u32[]{:S(2)}) async-start(bf16[128,2,128]{2,1,0:T(2,128)(2,1)} %bitcast.76), calls=%async_computation.1 | async-start | bytes 131072 | tf_op jit(solution)/shard_map/all_to_all | solution.py:78
  120.2 1.6 reshape.152
  121.8 1.9 fusion.6
  123.7 1.2 fusion.50
  124.9 6.7 %all-to-all-done.1 = bf16[128,2,128]{2,1,0:T(2,128)(2,1)} async-done(((bf16[128,2,128]{2,1,0:T(2,128)(2,1)}), bf16[128,2,128]{2,1,0:T(2,128)(2,1)}, u32[]{:S(2)}, u32[]{:S(2)}) %all-to-all-start.1) | async-done | bytes 65568 | tf_op jit(solution)/shard_map/all_to_all | solution.py:78
  132.6 2.1 fusion.7
  136.4 7.4 %all-to-all-start.5 = ((bf16[128,2,128]{2,1,0:T(2,128)(2,1)}), bf16[128,2,128]{2,1,0:T(2,128)(2,1)S(1)}, u32[]{:S(2)}, u32[]{:S(2)}) async-start(bf16[128,2,128]{2,1,0:T(2,128)(2,1)} %convert_element_type.92), calls=%async_computation.5 | async-start | bytes 131072 | tf_op jit(solution)/shard_map/all_to_all | solution.py:88
  143.8 2.7 fusion.18
  146.5 1.1 copy.69
  147.6 7.6 %all-to-all-done.5 = bf16[128,2,128]{2,1,0:T(2,128)(2,1)S(1)} async-done(((bf16[128,2,128]{2,1,0:T(2,128)(2,1)}), bf16[128,2,128]{2,1,0:T(2,128)(2,1)S(1)}, u32[]{:S(2)}, u32[]{:S(2)}) %all-to-all-start.5) | async-done | bytes 65568 | tf_op jit(solution)/shard_map/all_to_all | solution.py:88
  155.2 2.0 scatter_custom_fusion
  157.2 2.2 fusion.28
  159.4 3.3 %convolution_add_fusion = f32[512,512]{1,0:T(8,128)} fusion(f32[512,512]{1,0:T(8,128)} %fusion.28, bf16[512,512]{1,0:T(8,128)(2,1)} %param.24, bf16[512,512]{1,0:T(8,128)(2,1)S(1)} %fusion.11, bf16[512,512]{1,0:T(8,128)(2,1)} %param.23, f32[512,512]{1,0:T(8,128)S(1)} %fusion.55), kind=kOutput, calls=%fused_computation.12 | convolution fusion | flops 538705920 | bytes 4718592 | tf_op jit(solution)/shard_map/dot_general | solution.py:108
  165.3 18.2 %reduce-scatter.2.cloned.1.call-done = f32[128,512]{1,0:T(8,128)} async-done(((f32[512,512]{1,0:T(8,128)}), f32[128,512]{1,0:T(8,128)}) %reduce-scatter.2.cloned.1.call-update) | async-done | bytes 262160 | tf_op jit(solution)/shard_map/reduce_scatter | solution.py:107
  184.9 98.6 %psum.7 = f32[16,512]{1,0:T(8,128)S(1)} all-reduce(f32[16,512]{1,0:T(8,128)S(1)} %fusion.38), channel_id=1, replica_groups=mesh['round'=128,'mp'=4] {'round','mp'}, use_global_device_ids=true, to_apply=%region_8.9 | all-reduce | flops 8192 | bytes 65536 | tf_op jit(solution)/shard_map/psum | solution.py:123
  (60 shorter events, 17.2 us)
Async XLA Ops:
  7.2 20.7 %copy-start = (bf16[1,512,512]{2,1,0:T(8,128)(2,1)S(1)}, bf16[1,512,512]{2,1,0:T(8,128)(2,1)}, u32[]{:S(2)}) copy-start(bf16[1,512,512]{2,1,0:T(8,128)(2,1)} %param.13) | copy-start | bytes 1572868
  8.7 29.8 %all-to-all-start.2 = ((bf16[128,1,2]{2,1,0:T(2,128)(2,1)}), bf16[128,1,2]{2,1,0:T(2,128)(2,1)S(1)}, u32[]{:S(2)}, u32[]{:S(2)}) async-start(bf16[128,1,2]{2,1,0:T(2,128)(2,1)} %copy.61), calls=%async_computation.2 | async-start | bytes 131072 | tf_op jit(solution)/shard_map/all_to_all | solution.py:79
  35.0 14.9 %copy-start.6 = (s32[1,128,2]{1,2,0:T(2,128)S(1)}, s32[1,128,2]{1,2,0:T(2,128)}, u32[]{:S(2)}) copy-start(s32[1,128,2]{1,2,0:T(2,128)} %param.15) | copy-start | bytes 3076
  38.5 31.9 %all-to-all-start = ((bf16[128,2,1024]{2,1,0:T(2,128)(2,1)}), bf16[128,2,1024]{2,1,0:T(2,128)(2,1)S(1)}, u32[]{:S(2)}, u32[]{:S(2)}) async-start(bf16[128,2,1024]{2,1,0:T(2,128)(2,1)} %reshape.218), calls=%async_computation | async-start | bytes 1048576 | tf_op jit(solution)/shard_map/all_to_all | solution.py:56
  71.9 0.7 copy-start.7
  72.1 0.9 copy-start.3
  72.6 0.9 copy-start.4
  77.0 17.0 %all-to-all-start.3 = ((bf16[128,2,128]{2,1,0:T(2,128)(2,1)}), bf16[128,2,128]{2,1,0:T(2,128)(2,1)}, u32[]{:S(2)}, u32[]{:S(2)}) async-start(bf16[128,2,128]{2,1,0:T(2,128)(2,1)} %bitcast.12), calls=%async_computation.3 | async-start | bytes 131072 | tf_op jit(solution)/shard_map/all_to_all | solution.py:76
  83.3 1.5 copy-start.5
  94.1 19.2 %all-to-all-start.4 = ((bf16[128,2,128]{2,1,0:T(2,128)(2,1)}), bf16[128,2,128]{2,1,0:T(2,128)(2,1)}, u32[]{:S(2)}, u32[]{:S(2)}) async-start(bf16[128,2,128]{2,1,0:T(2,128)(2,1)} %bitcast.78), calls=%async_computation.4 | async-start | bytes 131072 | tf_op jit(solution)/shard_map/all_to_all | solution.py:77
  113.3 18.3 %all-to-all-start.1 = ((bf16[128,2,128]{2,1,0:T(2,128)(2,1)}), bf16[128,2,128]{2,1,0:T(2,128)(2,1)}, u32[]{:S(2)}, u32[]{:S(2)}) async-start(bf16[128,2,128]{2,1,0:T(2,128)(2,1)} %bitcast.76), calls=%async_computation.1 | async-start | bytes 131072 | tf_op jit(solution)/shard_map/all_to_all | solution.py:78
  136.4 18.8 %all-to-all-start.5 = ((bf16[128,2,128]{2,1,0:T(2,128)(2,1)}), bf16[128,2,128]{2,1,0:T(2,128)(2,1)S(1)}, u32[]{:S(2)}, u32[]{:S(2)}) async-start(bf16[128,2,128]{2,1,0:T(2,128)(2,1)} %convert_element_type.92), calls=%async_computation.5 | async-start | bytes 131072 | tf_op jit(solution)/shard_map/all_to_all | solution.py:88
  143.8 39.8 %reduce-scatter.2.cloned.1.call-start = ((), (), s32[]{:S(2)}) async-start(), calls=%async_computation.7 | async-start | bytes 1310720 | tf_op jit(solution)/shard_map/reduce_scatter | solution.py:107
  162.7 0.8 copy-start.2
  163.5 120.0 %copy-start.8 = (f32[512]{0:T(512)S(1)}, f32[512]{0:T(512)}, u32[]{:S(2)}) copy-start(f32[512]{0:T(512)} %param.25) | copy-start | bytes 6148
  184.6 99.6 %copy-start.1 = (bf16[32,4,512]{2,1,0:T(4,128)(2,1)}, bf16[32,4,512]{2,1,0:T(4,128)(2,1)S(1)}, u32[]{:S(2)}) copy-start(bf16[32,4,512]{2,1,0:T(4,128)(2,1)S(1)} %reshape.153) | copy-start | bytes 393220
Sparse Core Ops, SparseCore 0:
  162.9 20.6 reduce-scatter.1
where the time goes:
time: 292 us; the launch traced here: 291 us
  blocking collectives  98.6 us (34%)
  waiting for transfers between devices  68.8 us (24%)
  starting transfers between devices  58.4 us (20%)
  local copies, waits for them, and re-layouts  20.8 us (7%)
  matrix products  19.2 us (7%)
  between operations  14.4 us (5%)
  other arithmetic  10.9 us (4%)
    psum x1, blocking collectives, shards(): pooled = lax.psum(partial_sum, ('round', 'mp'))  98.6 us
    all_to_all x1, waiting for transfers between devices, shards(): lax.all_to_all(permuted, 'round', split_axis=1, concat_axis=0, tiled=True)  19.6 us
    all_to_all x1, starting transfers between devices, shards(): lax.all_to_all(live_slot.astype(jnp.bfloat16), 'round', split_axis=0, con...  18.4 us
    reduce_scatter x1, waiting for transfers between devices, shards(): lax.psum_scatter(attn_part + jnp.dot(hidden, w_down, preferred_element_ty...  18.2 us
    all_to_all x1, starting transfers between devices, shards(): lax.all_to_all(permuted, 'round', split_axis=1, concat_axis=0, tiled=True)  11.3 us
    all_to_all x1, waiting for transfers between devices, shards(): lax.all_to_all(keys_all[safe_rows], 'round', split_axis=0, concat_axis=0,...  8.46 us
    all_to_all x1, starting transfers between devices, shards(): lax.all_to_all(keys_all[safe_rows], 'round', split_axis=0, concat_axis=0,...  8.03 us
    all_to_all x1, waiting for transfers between devices, shards(): lax.all_to_all(seam_attn.reshape(round_count, -1, head_width), 'round', s...  7.59 us
  transfers between devices with their start and end apart: 7, of which 7 were waited for; matrix products, arithmetic and copies ran while one was open for 10% of the time, Pallas kernels for 0%

commit v1 on v0

--- a/solution.py
+++ b/solution.py
@@ -120,7 +120,7 @@
     )
     support_count = round_count * jnp.sum(obs_mask.astype(jnp.float32), axis=1)
     divisor = jnp.sqrt(support_count)
-    pooled = lax.psum(partial_sum, ("round", "mp"))
+    pooled = jnp.sum(lax.all_gather(partial_sum, ("round", "mp")), axis=0)
     obs_logits = jnp.dot(pooled, w_read, precision=lax.Precision.HIGHEST) / divisor
     return (tiles_out, obs_logits)
 

time: 292 us -> 342 us (1.17)
  waiting for transfers between devices: 68.8 us -> 208 us
  blocking collectives: 98.6 us -> 0 us
  other arithmetic: 10.9 us -> 18 us
    all_gather x0 -> x1, waiting for transfers between devices: none -> 140 us  [shards(): pooled = jnp.sum(lax.all_gather(partial_sum, ('round', 'mp')), axis=0)]
    psum x1 -> x0, blocking collectives: 98.6 us -> none  [shards(): pooled = lax.psum(partial_sum, ('round', 'mp'))]
    reduce_sum x0 -> x1, other arithmetic: none -> 6.78 us  [shards(): pooled = jnp.sum(lax.all_gather(partial_sum, ('round', 'mp')), axis=0)]
  transfers between devices with their start and end apart: 7 -> 8, of which waited for: 7 -> 8; matrix products, arithmetic and copies ran while one was open for 10% -> 9% of each run, Pallas kernels for 0% -> 0%
where the time goes in v1:
time: 342 us; the launch traced here: 341 us
  waiting for transfers between devices  208 us (61%)
  starting transfers between devices  61.6 us (18%)
  matrix products  19.8 us (6%)
  local copies, waits for them, and re-layouts  19.2 us (6%)
  other arithmetic  18 us (5%)
  between operations  14.4 us (4%)
    all_gather x1, waiting for transfers between devices, shards(): pooled = jnp.sum(lax.all_gather(partial_sum, ('round', 'mp')), axis=0)  140 us
    all_to_all x1, waiting for transfers between devices, shards(): lax.all_to_all(permuted, 'round', split_axis=1, concat_axis=0, tiled=True)  19.6 us
    reduce_scatter x1, waiting for transfers between devices, shards(): lax.psum_scatter(attn_part + jnp.dot(hidden, w_down, preferred_element_ty...  19.3 us
    all_to_all x1, starting transfers between devices, shards(): lax.all_to_all(live_slot.astype(jnp.bfloat16), 'round', split_axis=0, con...  18.4 us
    all_to_all x1, starting transfers between devices, shards(): lax.all_to_all(permuted, 'round', split_axis=1, concat_axis=0, tiled=True)  11.3 us
    all_to_all x1, starting transfers between devices, shards(): lax.all_to_all(keys_all[safe_rows], 'round', split_axis=0, concat_axis=0,...  10.8 us
    all_to_all x1, waiting for transfers between devices, shards(): lax.all_to_all(keys_all[safe_rows], 'round', split_axis=0, concat_axis=0,...  9.36 us
    all_to_all x1, starting transfers between devices, shards(): lax.all_to_all(seam_attn.reshape(round_count, -1, head_width), 'round', s...  7.86 us
  transfers between devices with their start and end apart: 8, of which 8 were waited for; matrix products, arithmetic and copies ran while one was open for 9% of the time, Pallas kernels for 0%

profile of v1, /device:TPU:1, one launch (start us, length us, event | category | flops | bytes accessed | tf_op | source)
XLA Modules:
  0.0 340.9 jit_solution(12342153771098729261)
XLA Ops:
  8.7 18.4 %all-to-all-start.2 = ((bf16[128,1,2]{2,1,0:T(2,128)(2,1)}), bf16[128,1,2]{2,1,0:T(2,128)(2,1)S(1)}, u32[]{:S(2)}, u32[]{:S(2)}) async-start(bf16[128,1,2]{2,1,0:T(2,128)(2,1)} %copy.61), calls=%async_computation.2 | async-start | bytes 131072 | tf_op jit(solution)/shard_map/all_to_all | solution.py:79
  27.8 2.0 gather_fusion
  31.1 3.8 %reduce.2 = bf16[512,512]{1,0:T(8,128)(2,1)S(1)} reduce(bf16[512,1,512]{2,1,0:T(2,128)(2,1)S(1)} %bitcast.71, bf16[]{:T(256)} %broadcast.153), dimensions={1}, to_apply=%bitcast.67.reduce_sub_computation | reduce | bytes 1048578
  35.0 1.1 reshape.219
  36.1 2.4 all-to-all-done.2
  38.5 11.3 %all-to-all-start = ((bf16[128,2,1024]{2,1,0:T(2,128)(2,1)}), bf16[128,2,1024]{2,1,0:T(2,128)(2,1)S(1)}, u32[]{:S(2)}, u32[]{:S(2)}) async-start(bf16[128,2,1024]{2,1,0:T(2,128)(2,1)} %reshape.219), calls=%async_computation | async-start | bytes 1048576 | tf_op jit(solution)/shard_map/all_to_all | solution.py:56
  50.8 19.6 %all-to-all-done = bf16[128,2,1024]{2,1,0:T(2,128)(2,1)S(1)} async-done(((bf16[128,2,1024]{2,1,0:T(2,128)(2,1)}), bf16[128,2,1024]{2,1,0:T(2,128)(2,1)S(1)}, u32[]{:S(2)}, u32[]{:S(2)}) %all-to-all-start) | async-done | bytes 524320 | tf_op jit(solution)/shard_map/all_to_all | solution.py:56
  70.9 1.1 bitcast_convert_fusion
  72.7 1.5 gather_fusion.2
  74.2 6.2 %all-to-all-start.3 = ((bf16[128,2,128]{2,1,0:T(2,128)(2,1)}), bf16[128,2,128]{2,1,0:T(2,128)(2,1)}, u32[]{:S(2)}, u32[]{:S(2)}) async-start(bf16[128,2,128]{2,1,0:T(2,128)(2,1)} %bitcast.12), calls=%async_computation.3 | async-start | bytes 131072 | tf_op jit(solution)/shard_map/all_to_all | solution.py:76
  80.9 1.5 gather_fusion.3
  82.4 1.5 fusion.55
  83.9 1.9 convolution_convert_fusion.2
  86.8 1.5 gather_fusion.1
  88.2 3.0 all-to-all-done.3
  91.3 10.8 %all-to-all-start.4 = ((bf16[128,2,128]{2,1,0:T(2,128)(2,1)}), bf16[128,2,128]{2,1,0:T(2,128)(2,1)}, u32[]{:S(2)}, u32[]{:S(2)}) async-start(bf16[128,2,128]{2,1,0:T(2,128)(2,1)} %bitcast.79), calls=%async_computation.4 | async-start | bytes 131072 | tf_op jit(solution)/shard_map/all_to_all | solution.py:77
  103.9 9.4 %all-to-all-done.4 = bf16[128,2,128]{2,1,0:T(2,128)(2,1)} async-done(((bf16[128,2,128]{2,1,0:T(2,128)(2,1)}), bf16[128,2,128]{2,1,0:T(2,128)(2,1)}, u32[]{:S(2)}, u32[]{:S(2)}) %all-to-all-start.4) | async-done | bytes 65568 | tf_op jit(solution)/shard_map/all_to_all | solution.py:77
  113.2 6.9 %all-to-all-start.1 = ((bf16[128,2,128]{2,1,0:T(2,128)(2,1)}), bf16[128,2,128]{2,1,0:T(2,128)(2,1)}, u32[]{:S(2)}, u32[]{:S(2)}) async-start(bf16[128,2,128]{2,1,0:T(2,128)(2,1)} %bitcast.78), calls=%async_computation.1 | async-start | bytes 131072 | tf_op jit(solution)/shard_map/all_to_all | solution.py:78
  120.1 1.6 reshape.152
  121.7 1.9 fusion.6
  123.6 1.2 fusion.50
  124.9 6.7 %all-to-all-done.1 = bf16[128,2,128]{2,1,0:T(2,128)(2,1)} async-done(((bf16[128,2,128]{2,1,0:T(2,128)(2,1)}), bf16[128,2,128]{2,1,0:T(2,128)(2,1)}, u32[]{:S(2)}, u32[]{:S(2)}) %all-to-all-start.1) | async-done | bytes 65568 | tf_op jit(solution)/shard_map/all_to_all | solution.py:78
  132.5 2.1 fusion.7
  136.3 7.9 %all-to-all-start.5 = ((bf16[128,2,128]{2,1,0:T(2,128)(2,1)}), bf16[128,2,128]{2,1,0:T(2,128)(2,1)}, u32[]{:S(2)}, u32[]{:S(2)}) async-start(bf16[128,2,128]{2,1,0:T(2,128)(2,1)} %convert_element_type.92), calls=%async_computation.5 | async-start | bytes 131072 | tf_op jit(solution)/shard_map/all_to_all | solution.py:88
  144.2 2.7 fusion.18
  148.0 7.3 %all-to-all-done.5 = bf16[128,2,128]{2,1,0:T(2,128)(2,1)} async-done(((bf16[128,2,128]{2,1,0:T(2,128)(2,1)}), bf16[128,2,128]{2,1,0:T(2,128)(2,1)}, u32[]{:S(2)}, u32[]{:S(2)}) %all-to-all-start.5) | async-done | bytes 65568 | tf_op jit(solution)/shard_map/all_to_all | solution.py:88
  155.3 2.3 scatter_custom_fusion
  157.7 2.2 fusion.28
  159.9 3.3 convolution_add_fusion
  165.0 19.3 %reduce-scatter.2.cloned.1.call-done = f32[128,512]{1,0:T(8,128)} async-done(((f32[512,512]{1,0:T(8,128)}), f32[128,512]{1,0:T(8,128)}) %reduce-scatter.2.cloned.1.call-update) | async-done | bytes 262160 | tf_op jit(solution)/shard_map/reduce_scatter | solution.py:107
  186.4 140.2 %all-gather.3.cloned.1.call-done = f32[8192,512]{1,0:T(8,128)} async-done(((f32[16,512]{1,0:T(8,128)}), f32[8192,512]{1,0:T(8,128)}) %all-gather.3.cloned.1.call-update) | async-done | bytes 16777232 | tf_op jit(solution)/shard_map/all_gather | solution.py:123
  326.6 6.8 %reduce_sum.59 = f32[16,512]{1,0:T(8,128)S(1)} reduce(f32[512,16,512]{2,1,0:T(8,128)} %bitcast.69, f32[]{:T(128)} %constant.20.clone.1), dimensions={0}, to_apply=%region_8.9 | reduce | flops 4186112 | bytes 16809988 | tf_op jit(solution)/shard_map/reduce_sum | solution.py:123
  (61 shorter events, 17.1 us)
Async XLA Ops:
  7.2 20.7 %copy-start = (bf16[1,512,512]{2,1,0:T(8,128)(2,1)S(1)}, bf16[1,512,512]{2,1,0:T(8,128)(2,1)}, u32[]{:S(2)}) copy-start(bf16[1,512,512]{2,1,0:T(8,128)(2,1)} %param.13) | copy-start | bytes 1572868
  8.7 29.8 %all-to-all-start.2 = ((bf16[128,1,2]{2,1,0:T(2,128)(2,1)}), bf16[128,1,2]{2,1,0:T(2,128)(2,1)S(1)}, u32[]{:S(2)}, u32[]{:S(2)}) async-start(bf16[128,1,2]{2,1,0:T(2,128)(2,1)} %copy.61), calls=%async_computation.2 | async-start | bytes 131072 | tf_op jit(solution)/shard_map/all_to_all | solution.py:79
  30.6 19.2 %copy-start.5 = (s32[1,128,2]{1,2,0:T(2,128)S(1)}, s32[1,128,2]{1,2,0:T(2,128)}, u32[]{:S(2)}) copy-start(s32[1,128,2]{1,2,0:T(2,128)} %param.15) | copy-start | bytes 3076
  38.5 31.9 %all-to-all-start = ((bf16[128,2,1024]{2,1,0:T(2,128)(2,1)}), bf16[128,2,1024]{2,1,0:T(2,128)(2,1)S(1)}, u32[]{:S(2)}, u32[]{:S(2)}) async-start(bf16[128,2,1024]{2,1,0:T(2,128)(2,1)} %reshape.219), calls=%async_computation | async-start | bytes 1048576 | tf_op jit(solution)/shard_map/all_to_all | solution.py:56
  50.8 21.4 %copy-start.6 = (f32[512]{0:T(512)S(1)}, f32[512]{0:T(512)}, u32[]{:S(2)}) copy-start(f32[512]{0:T(512)} %param.17) | copy-start | bytes 6148
  70.9 1.4 copy-start.3
  72.0 8.5 %copy-start.4 = (bf16[512,128]{1,0:T(8,128)(2,1)S(1)}, bf16[512,128]{1,0:T(8,128)(2,1)}, u32[]{:S(2)}) copy-start(bf16[512,128]{1,0:T(8,128)(2,1)} %param.19) | copy-start | bytes 393220
  74.2 17.1 %all-to-all-start.3 = ((bf16[128,2,128]{2,1,0:T(2,128)(2,1)}), bf16[128,2,128]{2,1,0:T(2,128)(2,1)}, u32[]{:S(2)}, u32[]{:S(2)}) async-start(bf16[128,2,128]{2,1,0:T(2,128)(2,1)} %bitcast.12), calls=%async_computation.3 | async-start | bytes 131072 | tf_op jit(solution)/shard_map/all_to_all | solution.py:76
  91.3 22.0 %all-to-all-start.4 = ((bf16[128,2,128]{2,1,0:T(2,128)(2,1)}), bf16[128,2,128]{2,1,0:T(2,128)(2,1)}, u32[]{:S(2)}, u32[]{:S(2)}) async-start(bf16[128,2,128]{2,1,0:T(2,128)(2,1)} %bitcast.79), calls=%async_computation.4 | async-start | bytes 131072 | tf_op jit(solution)/shard_map/all_to_all | solution.py:77
  113.2 18.3 %all-to-all-start.1 = ((bf16[128,2,128]{2,1,0:T(2,128)(2,1)}), bf16[128,2,128]{2,1,0:T(2,128)(2,1)}, u32[]{:S(2)}, u32[]{:S(2)}) async-start(bf16[128,2,128]{2,1,0:T(2,128)(2,1)} %bitcast.78), calls=%async_computation.1 | async-start | bytes 131072 | tf_op jit(solution)/shard_map/all_to_all | solution.py:78
  136.3 19.0 %all-to-all-start.5 = ((bf16[128,2,128]{2,1,0:T(2,128)(2,1)}), bf16[128,2,128]{2,1,0:T(2,128)(2,1)}, u32[]{:S(2)}, u32[]{:S(2)}) async-start(bf16[128,2,128]{2,1,0:T(2,128)(2,1)} %convert_element_type.92), calls=%async_computation.5 | async-start | bytes 131072 | tf_op jit(solution)/shard_map/all_to_all | solution.py:88
  144.2 40.1 %reduce-scatter.2.cloned.1.call-start = ((), (), s32[]{:S(2)}) async-start(), calls=%async_computation.7 | async-start | bytes 1310720 | tf_op jit(solution)/shard_map/reduce_scatter | solution.py:107
  159.9 3.4 copy-start.2
  163.2 163.4 %all-gather.3.cloned.1.call-start = ((), (), s32[]{:S(2)}) async-start(), calls=%async_computation.8 | async-start | bytes 16809984 | tf_op jit(solution)/shard_map/all_gather | solution.py:123
  185.3 148.1 %copy-start.1 = (bf16[32,4,512]{2,1,0:T(4,128)(2,1)}, bf16[32,4,512]{2,1,0:T(4,128)(2,1)S(1)}, u32[]{:S(2)}) copy-start(bf16[32,4,512]{2,1,0:T(4,128)(2,1)S(1)} %reshape.153) | copy-start | bytes 393220
  326.6 6.8 %copy-start.7 = (f32[512]{0:T(512)S(1)}, f32[512]{0:T(512)}, u32[]{:S(2)}) copy-start(f32[512]{0:T(512)} %param.25) | copy-start | bytes 6148
Sparse Core Ops, SparseCore 0:
  163.3 20.9 reduce-scatter.1
  189.7 136.8 all-gather.2
